TPU v7x, 32 devices: a whole 2x2x4 slice. The times are simulated.
32 devices in a mesh: fsdp: 8 (over y, x, core), mode: 4 (over z).
Axes of the slice: x: 2, y: 2, z: 4, core: 2. Of those that a mesh axis runs over, the one named last changes fastest.
Arguments:
- gradient: float32 [32, 16, 2, 256, 512], P('mode', None, None, 'fsdp'), may hold values from -1000 to 1000, as said below
- start_in: float32 [512, 128], replicated, may hold values from -6 to 6
- start_out: float32 [256, 128], replicated, may hold values from -6 to 6
- start_x: float32 [32, 16], replicated, may hold values from -6 to 6
- start_y: float32 [16, 8], replicated, may hold values from -6 to 6
Outputs:
- factor_in: float32 [512, 128], P(('fsdp', 'mode'))
- factor_out: float32 [256, 128], P('fsdp')
- factor_x: float32 [32, 16], replicated
- factor_y: float32 [16, 8], replicated
- core: float32 [16, 128, 8, 2, 128], P('mode', 'fsdp')
Inputs may be any that keep to these rules, and one draw needn't show every extreme that they name: A weight gradient of one spectral layer, finite and bounded in magnitude.
All inputs are finite; a program needn't handle non-finite values.
Results may differ from a plain program's by a relative error of at most 0.0003.
Values sent between devices are 32-bit elements; how exact they have to be, the bound alone decides.
No kernel may reach another device: no remote copies, remote signals or barrier semaphores. Data moves between devices by JAX's collectives and lax.ppermute only.
A program may use at most 320 MiB of HBM per device.

v0:
```python
import jax
import jax.numpy as jnp
from jax import lax
from jax.sharding import PartitionSpec as P

I = 512
SWEEPS = 2
precise = lax.Precision.HIGHEST


def sweeps(gram, subspace):
    for sweep_index in range(SWEEPS):
        product = jnp.dot(gram, subspace, precision=precise)
        inner = jnp.dot(product.T, product, precision=precise)
        lower_factor = jnp.linalg.cholesky(inner)
        subspace = jax.scipy.linalg.solve_triangular(lower_factor, product.T, lower=True).T
    return subspace


def shards(gradient, start_in, start_out, start_x, start_y):
    fsdp_index = lax.axis_index("fsdp")
    mode_index = lax.axis_index("mode")
    joint_index = lax.axis_index(("fsdp", "mode"))
    fsdp_count = lax.axis_size("fsdp")
    mode_count = lax.axis_size("mode")
    rows_in = I // (fsdp_count * mode_count)
    local_first = gradient.shape[0]
    local_out = gradient.shape[3]
    gram_y_part = jnp.einsum("xycoi,xzcoi->yz", gradient, gradient, precision=precise)
    gram_in_part = jnp.einsum("xycoi,xycoj->ij", gradient, gradient, precision=precise)
    gram_in, gram_y = lax.psum((gram_in_part, gram_y_part), ("fsdp", "mode"))
    full_in = sweeps(gram_in, start_in)
    factor_y = sweeps(gram_y, start_y)
    by_out = lax.all_to_all(gradient, "fsdp", split_axis=4, concat_axis=3, tiled=True)
    gram_out = lax.psum(
        jnp.einsum("xycoi,xycpi->op", by_out, by_out, precision=precise), ("fsdp", "mode")
    )
    by_first = lax.all_to_all(gradient, "mode", split_axis=4, concat_axis=0, tiled=True)
    gram_x = lax.psum(
        jnp.einsum("xycoi,zycoi->xz", by_first, by_first, precision=precise), ("fsdp", "mode")
    )
    full_out = sweeps(gram_out, start_out)
    factor_x = sweeps(gram_x, start_x)
    partial_in = jnp.einsum("xycoi,ia->xycoa", gradient, full_in, precision=precise)
    out_rows = lax.dynamic_slice_in_dim(full_out, fsdp_index * local_out, local_out, 0)
    first_rows = lax.dynamic_slice_in_dim(factor_x, mode_index * local_first, local_first, 0)
    reduced = jnp.einsum("xycoa,yq->xqcoa", partial_in, factor_y, precision=precise)
    columns = first_rows
    partial_core = lax.psum_scatter(
        jnp.einsum("xqcoa,xp->pqcoa", reduced, columns, precision=precise),
        "mode",
        scatter_dimension=0,
        tiled=True,
    )
    columns = out_rows
    swapped = lax.psum_scatter(
        jnp.einsum("pqcoa,ob->bpqca", partial_core, columns, precision=precise),
        "fsdp",
        scatter_dimension=0,
        tiled=True,
    )
    core = jnp.transpose(swapped, (1, 0, 2, 3, 4))
    factor_in = lax.dynamic_slice_in_dim(full_in, joint_index * rows_in, rows_in, 0)
    return (factor_in, out_rows, factor_x, factor_y, core)


def solution(mesh):
    in_specs = (P("mode", None, None, "fsdp", None), P(), P(), P(), P())
    out_specs = (
        P(("fsdp", "mode"), None),
        P("fsdp", None),
        P(),
        P(),
        P("mode", "fsdp", None, None, None),
    )
    return jax.shard_map(shards, mesh=mesh, in_specs=in_specs, out_specs=out_specs, check_vma=False)
```

profile of v0, /device:TPU:0, one launch (start us, length us, event | category | flops | bytes accessed | tf_op | source)
XLA Modules:
  0.0 1270.9 jit_solution(15433066055648959006)
XLA Ops:
  7.2 50.4 %copy.78 = f32[8,16,2,32,512]{3,1,2,0,4:T(8,128)} copy(f32[8,16,2,32,512]{4,3,2,1,0:T(8,128)} %param.16) | data formatting | bytes 33554432 | tf_op args[0]
  57.6 67.0 %reshape.45 = f32[8,1,524288]{2,1,0:T(1,128)} reshape(f32[512,8,2,16,32]{4,3,2,1,0:T(8,128)} %bitcast.156) | data formatting | bytes 33554432
  124.6 5.7 all-to-all-start
  130.3 60.2 %reshape.47 = f32[4,1,1048576]{2,1,0:T(1,128)} reshape(f32[512,8,2,16,32]{4,3,2,1,0:T(8,128)} %bitcast.158) | data formatting | bytes 33554432
  190.5 124.4 %all-to-all-done = f32[8,1,524288]{2,1,0:T(1,128)} async-done(((f32[8,1,524288]{2,1,0:T(1,128)}), f32[8,1,524288]{2,1,0:T(1,128)}, u32[]{:S(2)}, u32[]{:S(2)}) %all-to-all-start) | async-done | bytes 16777248 | tf_op jit(solution)/shard_map/all_to_all | solution.py:34
  314.9 7.2 all-to-all-start.1
  322.2 31.6 %fusion.13 = f32[512,512]{1,0:T(8,128)} fusion(f32[8,16,2,32,512]{4,3,2,1,0:T(8,128)} %param.16), kind=kOutput, calls=%fused_computation.12 | convolution fusion | flops 25769803776 | bytes 17825792 | tf_op jit(solution)/shard_map/xycoi,xycoj->ij/dot_general | solution.py:30
  354.3 50.6 %reduce.12 = f32[8,524288]{1,0:T(8,128)} reduce(f32[8,1,524288]{2,1,0:T(1,128)} %all-to-all-done, f32[]{:T(128)} %broadcast.120), dimensions={1}, to_apply=%all_to_all.26.reduce_sub_computation | reduce | bytes 33554436 | tf_op jit(solution)/shard_map/all_to_all | solution.py:34
  404.9 55.4 %reshape.46 = f32[512,8,2,16,32]{4,3,2,1,0:T(8,128)} reshape(f32[8,524288]{1,0:T(8,128)} %reduce.12) | data formatting | bytes 33554432
  460.3 48.4 %copy.113 = f32[8,16,2,32,8,64]{5,3,4,1,0,2:T(8,128)} copy(f32[8,16,2,32,8,64]{3,1,2,0,5,4:T(8,128)} %bitcast.11) | data formatting | bytes 33554432 | tf_op jit(solution)/shard_map/all_to_all | solution.py:34
  508.7 36.8 %convolution_bitcast_fusion.1 = f32[256,256]{1,0:T(8,128)} fusion(f32[8,16,2,256,64]{4,3,1,0,2:T(8,128)} %bitcast.196), kind=kOutput, calls=%fused_computation.13 | convolution fusion | flops 12884901888 | bytes 17039360 | tf_op jit(solution)/shard_map/xycoi,xycpi->op/dot_general | solution.py:36
  545.6 51.9 %fusion.19 = f32[16,16]{1,0:T(8,128)S(1)} fusion(f32[8,16,2,32,512]{4,3,2,1,0:T(8,128)} %param.16), kind=kOutput, calls=%fused_computation.15 | convolution fusion | flops 805306368 | bytes 16778240 | tf_op jit(solution)/shard_map/xycoi,xzcoi->yz/dot_general | solution.py:29
  597.5 196.5 %all-reduce.4.cloned.1.call-done = (f32[512,512]{1,0:T(8,128)}, f32[256,256]{1,0:T(8,128)}) async-done(((f32[512,512]{1,0:T(8,128)}, f32[256,256]{1,0:T(8,128)}), (f32[512,512]{1,0:T(8,128)}, f32[256,256]{1,0:T(8,128)})) %all-reduce.4.cloned.1.call-update) | async-done | bytes 1310736 | tf_op jit(solution)/shard_map/psum | solution.py:31
  794.0 2.2 fusion.77
  796.9 11.7 cholesky.158
  809.3 0.7 fusion.31
  810.0 9.8 custom-call.22
  820.2 2.2 fusion.79
  823.2 11.9 cholesky.169
  835.7 0.7 fusion.32
  836.4 9.8 custom-call.23
  846.6 17.3 %convolution_bitcast_fusion = f32[8,16,2,32,128]{4,3,2,1,0:T(8,128)} fusion(f32[8,16,2,32,512]{4,3,2,1,0:T(8,128)} %param.16, f32[128,512]{1,0:T(8,128)S(1)} %fusion.23), kind=kOutput, calls=%fused_computation.8 | convolution fusion | flops 6442450944 | bytes 21233664 | tf_op jit(solution)/shard_map/xycoi,ia->xycoa/dot_general | solution.py:44
  864.0 54.5 %reduce.13 = f32[4,1048576]{1,0:T(4,128)} reduce(f32[4,1,1048576]{2,1,0:T(1,128)} %all-to-all-done.1, f32[]{:T(128)} %broadcast.120), dimensions={1}, to_apply=%all_to_all.30.reduce_sub_computation | reduce | bytes 33554436 | tf_op jit(solution)/shard_map/all_to_all | solution.py:38
  918.5 76.0 %reshape.48 = f32[512,8,2,16,32]{4,3,2,1,0:T(8,128)} reshape(f32[4,1048576]{1,0:T(4,128)} %reduce.13) | data formatting | bytes 33554432
  994.5 42.8 %copy.85 = f32[8,16,2,32,4,128]{5,0,4,1,3,2:T(8,128)} copy(f32[8,16,2,32,4,128]{3,1,2,0,5,4:T(8,128)} %bitcast.26) | data formatting | bytes 33554432 | tf_op jit(solution)/shard_map/all_to_all | solution.py:38
  1037.3 19.6 %fusion.16 = f32[32,32]{1,0:T(8,128)S(1)} fusion(f32[8,16,2,32,4,128]{5,0,4,1,3,2:T(8,128)} %copy.85), kind=kOutput, calls=%fused_computation.14 | convolution fusion | flops 1610612736 | bytes 16781312 | tf_op jit(solution)/shard_map/xycoi,zycoi->xz/dot_general | solution.py:40
  1057.0 39.5 %all-reduce = (f32[32,32]{1,0:T(8,128)S(1)}, f32[16,16]{1,0:T(8,128)S(1)}) all-reduce(f32[32,32]{1,0:T(8,128)S(1)} %fusion.16, f32[16,16]{1,0:T(8,128)S(1)} %fusion.19), channel_id=1, replica_groups=mesh['fsdp'=8,'mode'=4] {'fsdp','mode'}, use_global_device_ids=true, to_apply=%region_4.8 | all-reduce | flops 1280 | bytes 10240 | tf_op jit(solution)/shard_map/psum | solution.py:39
  1096.8 0.7 cholesky.224
  1100.1 0.7 cholesky.235
  1103.3 1.5 cholesky.202
  1105.5 0.6 fusion.48
  1106.2 1.2 custom-call.26
  1108.0 1.5 cholesky.213
  1110.8 1.2 custom-call.27
  1112.2 6.9 fusion.10
  1119.1 4.2 fusion.8
  1123.3 3.2 copy.97
  1127.7 11.7 cholesky.180
  1140.1 0.7 fusion.33
  1140.8 9.8 custom-call.24
  1151.8 11.7 cholesky.191
  1164.2 0.7 fusion.34
  1164.9 10.0 custom-call.25
  1175.2 28.3 %reduce-scatter.3.cloned.1.call-done = f32[4,8,2,32,128]{4,3,2,1,0:T(8,128)} async-done(((f32[16,8,2,32,128]{4,3,2,1,0:T(8,128)}), f32[4,8,2,32,128]{4,3,2,1,0:T(8,128)}) %reduce-scatter.3.cloned.1.call-update) | async-done | bytes 1048592 | tf_op jit(solution)/shard_map/reduce_scatter | solution.py:49
  1203.4 6.6 fusion.45
  1210.2 0.7 copy.98
  1211.5 50.3 %reduce-scatter.5.cloned.1.call-done = f32[16,4,8,2,128]{4,0,3,2,1:T(8,128)} async-done(((f32[128,4,8,2,128]{4,0,3,2,1:T(8,128)}), f32[16,4,8,2,128]{4,0,3,2,1:T(8,128)}) %reduce-scatter.5.cloned.1.call-update) | async-done | bytes 524304 | tf_op jit(solution)/shard_map/reduce_scatter | solution.py:56
  1261.8 2.1 copy.99
  (83 shorter events, 17.0 us)
Async XLA Ops:
  7.2 786.8 %copy-start = (f32[512,128]{1,0:T(8,128)S(1)}, f32[512,128]{1,0:T(8,128)}, u32[]{:S(2)}) copy-start(f32[512,128]{1,0:T(8,128)} %param.17) | copy-start | bytes 786436
  124.6 190.3 %all-to-all-start = ((f32[8,1,524288]{2,1,0:T(1,128)}), f32[8,1,524288]{2,1,0:T(1,128)}, u32[]{:S(2)}, u32[]{:S(2)}) async-start(f32[8,1,524288]{2,1,0:T(1,128)} %reshape.45), calls=%async_computation | async-start | bytes 33554432 | tf_op jit(solution)/shard_map/all_to_all | solution.py:34
  314.9 549.1 %all-to-all-start.1 = ((f32[4,1,1048576]{2,1,0:T(1,128)}), f32[4,1,1048576]{2,1,0:T(1,128)}, u32[]{:S(2)}, u32[]{:S(2)}) async-start(f32[4,1,1048576]{2,1,0:T(1,128)} %reshape.47), calls=%async_computation.1 | async-start | bytes 33554432 | tf_op jit(solution)/shard_map/all_to_all | solution.py:38
  322.1 471.9 %all-reduce.4.cloned.1.call-start = ((), (), s32[]{:S(2)}) async-start(), calls=%async_computation.6 | async-start | bytes 2621440 | tf_op jit(solution)/shard_map/psum | solution.py:31
  545.5 657.9 %reduce-scatter.3.cloned.1.call-start = ((), (), s32[]{:S(2)}) async-start(), calls=%async_computation.4 | async-start | bytes 5242880 | tf_op jit(solution)/shard_map/reduce_scatter | solution.py:49
  1037.3 59.2 %copy-start.6 = (f32[16,8]{0,1:T(8,128)S(1)}, f32[16,8]{0,1:T(8,128)}, u32[]{:S(2)}) copy-start(f32[16,8]{0,1:T(8,128)} %param.20) | copy-start | bytes 1540
  1037.3 65.7 %copy-start.5 = (f32[32,16]{0,1:T(8,128)S(1)}, f32[32,16]{0,1:T(8,128)}, u32[]{:S(2)}) copy-start(f32[32,16]{0,1:T(8,128)} %param.19) | copy-start | bytes 6148
  1056.9 69.9 %copy-start.1 = (f32[256,256]{1,0:T(8,128)S(1)}, f32[256,256]{1,0:T(8,128)}, u32[]{:S(2)}) copy-start(f32[256,256]{1,0:T(8,128)} %get-tuple-element.35) | copy-start | bytes 786436
  1057.0 69.9 %copy-start.2 = (f32[256,128]{1,0:T(8,128)S(1)}, f32[256,128]{1,0:T(8,128)}, u32[]{:S(2)}) copy-start(f32[256,128]{1,0:T(8,128)} %param.18) | copy-start | bytes 393220
  1103.0 107.1 %copy-start.4 = (f32[8,16]{1,0:T(8,128)}, f32[8,16]{1,0:T(8,128)S(1)}, u32[]{:S(2)}) copy-start(f32[8,16]{1,0:T(8,128)S(1)} %fusion.64) | copy-start | bytes 1540
  1112.2 97.9 %copy-start.3 = (f32[16,32]{1,0:T(8,128)}, f32[16,32]{1,0:T(8,128)S(1)}, u32[]{:S(2)}) copy-start(f32[16,32]{1,0:T(8,128)S(1)} %fusion.51) | copy-start | bytes 6148
  1126.5 135.2 %reduce-scatter.5.cloned.1.call-start = ((), (), s32[]{:S(2)}) async-start(), calls=%async_computation.5 | async-start | bytes 4718592 | tf_op jit(solution)/shard_map/reduce_scatter | solution.py:56
Sparse Core Ops, SparseCore 0:
  545.6 248.3 all-reduce.3
  1126.7 76.7 reduce-scatter.2
  1210.2 51.5 reduce-scatter.4
where the time goes:
time: 1280 us; the launch traced here: 1270 us
  local copies, waits for them, and re-layouts  408 us (32%)
  waiting for transfers between devices  400 us (31%)
  other arithmetic  210 us (16%)
  matrix products  185 us (14%)
  blocking collectives  39.5 us (3%)
  between operations  14.6 us (1%)
  starting transfers between devices  13.3 us (1%)
    unnamed x21, local copies, waits for them, and re-layouts  312 us
    psum x1, waiting for transfers between devices, shards(): gram_in, gram_y = lax.psum((gram_in_part, gram_y_part), ('fsdp', 'mode'))  197 us
    all_to_all x1, waiting for transfers between devices, shards(): lax.all_to_all(gradient, 'fsdp', split_axis=4, concat_axis=3, tiled=True)  124 us
    another operation x24, other arithmetic, sweeps(): lower_factor = jnp.linalg.cholesky(inner)  56.9 us
    all_to_all x1, other arithmetic, shards(): lax.all_to_all(gradient, 'mode', split_axis=4, concat_axis=0, tiled=True)  54.5 us
    dot_general x1, matrix products, shards(): jnp.einsum('xycoi,xzcoi->yz', gradient, gradient, precision=precise)  51.9 us
    all_to_all x1, other arithmetic, shards(): lax.all_to_all(gradient, 'fsdp', split_axis=4, concat_axis=3, tiled=True)  50.6 us
    reduce_scatter x1, waiting for transfers between devices, shards(): lax.psum_scatter(jnp.einsum('pqcoa,ob->bpqca', partial_core, columns, pre...  50.3 us
  transfers between devices with their start and end apart: 5, of which 4 were waited for; matrix products, arithmetic and copies ran while one was open for 36% of the time, Pallas kernels for 0%

commit v1 on v0

--- a/solution.py
+++ b/solution.py
@@ -6,6 +6,14 @@
 I = 512
 SWEEPS = 2
 precise = lax.Precision.HIGHEST
+
+
+def pages_balance(x_local):
+    mesh_ax = "mode"
+    row_axis = "fsdp"
+    for p in (mesh_ax, row_axis):
+        x_local = lax.psum(x_local, axis_name=p)
+    return x_local
 
 
 def sweeps(gram, subspace):
@@ -28,7 +36,7 @@
     local_out = gradient.shape[3]
     gram_y_part = jnp.einsum("xycoi,xzcoi->yz", gradient, gradient, precision=precise)
     gram_in_part = jnp.einsum("xycoi,xycoj->ij", gradient, gradient, precision=precise)
-    gram_in, gram_y = lax.psum((gram_in_part, gram_y_part), ("fsdp", "mode"))
+    gram_in, gram_y = pages_balance((gram_in_part, gram_y_part))
     full_in = sweeps(gram_in, start_in)
     factor_y = sweeps(gram_y, start_y)
     by_out = lax.all_to_all(gradient, "fsdp", split_axis=4, concat_axis=3, tiled=True)

time: 1280 us -> 1460 us (1.14)
  blocking collectives: 39.5 us -> 276 us
  waiting for transfers between devices: 400 us -> 344 us
    psum x0 -> x2, blocking collectives: none -> 237 us  [pages_balance(): x_local = lax.psum(x_local, axis_name=p)]
    psum x1 -> x3, waiting for transfers between devices: 197 us -> 143 us  [the longest x2 143 us: pages_balance(): x_local = lax.psum(x_local, axis_name=p)]
    unnamed x21 -> x23, local copies, waits for them, and re-layouts: 312 us -> 313 us
  transfers between devices with their start and end apart: 5 -> 7, of which waited for: 4 -> 4; matrix products, arithmetic and copies ran while one was open for 36% -> 47% of each run, Pallas kernels for 0% -> 0%
where the time goes in v1:
time: 1460 us; the launch traced here: 1450 us
  local copies, waits for them, and re-layouts  410 us (28%)
  waiting for transfers between devices  344 us (24%)
  blocking collectives  276 us (19%)
  other arithmetic  210 us (14%)
  matrix products  184 us (13%)
  between operations  16.1 us (1%)
    unnamed x23, local copies, waits for them, and re-layouts  313 us
    psum x2, blocking collectives, pages_balance(): x_local = lax.psum(x_local, axis_name=p)  237 us
    psum x2, waiting for transfers between devices, pages_balance(): x_local = lax.psum(x_local, axis_name=p)  143 us
    all_to_all x1, waiting for transfers between devices, shards(): lax.all_to_all(gradient, 'fsdp', split_axis=4, concat_axis=3, tiled=True)  124 us
    another operation x24, other arithmetic, sweeps(): lower_factor = jnp.linalg.cholesky(inner)  57 us
    all_to_all x1, other arithmetic, shards(): lax.all_to_all(gradient, 'mode', split_axis=4, concat_axis=0, tiled=True)  54.2 us
    dot_general x1, matrix products, shards(): jnp.einsum('xycoi,xzcoi->yz', gradient, gradient, precision=precise)  51.8 us
    all_to_all x1, other arithmetic, shards(): lax.all_to_all(gradient, 'fsdp', split_axis=4, concat_axis=3, tiled=True)  50.2 us
  transfers between devices with their start and end apart: 7, of which 4 were waited for; matrix products, arithmetic and copies ran while one was open for 47% of the time, Pallas kernels for 0%

profile of v1, /device:TPU:0, one launch (start us, length us, event | category | flops | bytes accessed | tf_op | source)
XLA Modules:
  0.0 1453.4 jit_solution(9082057743548179306)
XLA Ops:
  8.0 50.4 %copy.78 = f32[8,16,2,32,512]{3,1,2,0,4:T(8,128)} copy(f32[8,16,2,32,512]{4,3,2,1,0:T(8,128)} %param.16) | data formatting | bytes 33554432 | tf_op args[0]
  58.4 67.0 %reshape.45 = f32[8,1,524288]{2,1,0:T(1,128)} reshape(f32[512,8,2,16,32]{4,3,2,1,0:T(8,128)} %bitcast.156) | data formatting | bytes 33554432
  125.4 5.7 all-to-all-start
  131.2 60.2 %reshape.47 = f32[4,1,1048576]{2,1,0:T(1,128)} reshape(f32[512,8,2,16,32]{4,3,2,1,0:T(8,128)} %bitcast.158) | data formatting | bytes 33554432
  191.3 124.4 %all-to-all-done = f32[8,1,524288]{2,1,0:T(1,128)} async-done(((f32[8,1,524288]{2,1,0:T(1,128)}), f32[8,1,524288]{2,1,0:T(1,128)}, u32[]{:S(2)}, u32[]{:S(2)}) %all-to-all-start) | async-done | bytes 16777248 | tf_op jit(solution)/shard_map/all_to_all | solution.py:42
  315.8 7.2 all-to-all-start.1
  323.0 31.6 %fusion.13 = f32[512,512]{1,0:T(8,128)} fusion(f32[8,16,2,32,512]{4,3,2,1,0:T(8,128)} %param.16), kind=kOutput, calls=%fused_computation.12 | convolution fusion | flops 25769803776 | bytes 17825792 | tf_op jit(solution)/shard_map/xycoi,xycoj->ij/dot_general | solution.py:38
  355.1 51.8 %fusion.19 = f32[16,16]{1,0:T(8,128)S(1)} fusion(f32[8,16,2,32,512]{4,3,2,1,0:T(8,128)} %param.16), kind=kOutput, calls=%fused_computation.15 | convolution fusion | flops 805306368 | bytes 16778240 | tf_op jit(solution)/shard_map/xycoi,xzcoi->yz/dot_general | solution.py:37
  406.9 222.9 %psum.46 = f32[16,16]{1,0:T(8,128)S(1)} all-reduce(f32[16,16]{1,0:T(8,128)S(1)} %fusion.19), channel_id=1, replica_groups=mesh['fsdp'=8,'mode'=4] {'mode'}, use_global_device_ids=true, to_apply=%region_8.14 | all-reduce | flops 256 | bytes 2048 | tf_op jit(solution)/shard_map/psum | solution.py:15
  629.7 13.8 psum.47
  643.9 0.7 cholesky.224
  647.1 0.7 cholesky.235
  650.3 143.1 %all-reduce.6.cloned.1.call-done = f32[512,512]{1,0:T(8,128)} async-done(((f32[512,512]{1,0:T(8,128)}), f32[512,512]{1,0:T(8,128)}) %all-reduce.6.cloned.1.call-update) | async-done | bytes 1048592 | tf_op jit(solution)/shard_map/psum | solution.py:15
  793.4 2.2 fusion.77
  796.3 11.7 cholesky.158
  809.4 9.8 custom-call.22
  819.6 2.2 fusion.79
  822.5 12.1 cholesky.169
  836.0 9.8 custom-call.23
  846.2 0.7 copy-done.2
  846.9 16.6 %convolution_bitcast_fusion = f32[8,16,2,32,128]{4,3,2,1,0:T(8,128)S(1)} fusion(f32[8,16,2,32,512]{4,3,2,1,0:T(8,128)} %param.16, f32[128,512]{1,0:T(8,128)S(1)} %fusion.23), kind=kOutput, calls=%fused_computation.8 | convolution fusion | flops 6442450944 | bytes 21233664 | tf_op jit(solution)/shard_map/xycoi,ia->xycoa/dot_general | solution.py:52
  863.5 4.4 fusion.10
  868.4 50.2 %reduce.12 = f32[8,524288]{1,0:T(8,128)} reduce(f32[8,1,524288]{2,1,0:T(1,128)} %all-to-all-done, f32[]{:T(128)} %broadcast.120), dimensions={1}, to_apply=%all_to_all.26.reduce_sub_computation | reduce | bytes 33554436 | tf_op jit(solution)/shard_map/all_to_all | solution.py:42
  918.6 55.4 %reshape.46 = f32[512,8,2,16,32]{4,3,2,1,0:T(8,128)} reshape(f32[8,524288]{1,0:T(8,128)} %reduce.12) | data formatting | bytes 33554432
  974.1 48.4 %copy.113 = f32[8,16,2,32,8,64]{5,3,4,1,0,2:T(8,128)} copy(f32[8,16,2,32,8,64]{3,1,2,0,5,4:T(8,128)} %bitcast.11) | data formatting | bytes 33554432 | tf_op jit(solution)/shard_map/all_to_all | solution.py:42
  1022.5 36.8 %convolution_bitcast_fusion.1 = f32[256,256]{1,0:T(8,128)} fusion(f32[8,16,2,256,64]{4,3,1,0,2:T(8,128)} %bitcast.196), kind=kOutput, calls=%fused_computation.13 | convolution fusion | flops 12884901888 | bytes 17039360 | tf_op jit(solution)/shard_map/xycoi,xycpi->op/dot_general | solution.py:44
  1059.3 54.2 %reduce.13 = f32[4,1048576]{1,0:T(4,128)} reduce(f32[4,1,1048576]{2,1,0:T(1,128)} %all-to-all-done.1, f32[]{:T(128)} %broadcast.120), dimensions={1}, to_apply=%all_to_all.30.reduce_sub_computation | reduce | bytes 33554436 | tf_op jit(solution)/shard_map/all_to_all | solution.py:46
  1113.5 76.3 %reshape.48 = f32[512,8,2,16,32]{4,3,2,1,0:T(8,128)} reshape(f32[4,1048576]{1,0:T(4,128)} %reduce.13) | data formatting | bytes 33554432
  1189.9 42.8 %copy.85 = f32[8,16,2,32,4,128]{5,0,4,1,3,2:T(8,128)} copy(f32[8,16,2,32,4,128]{3,1,2,0,5,4:T(8,128)} %bitcast.26) | data formatting | bytes 33554432 | tf_op jit(solution)/shard_map/all_to_all | solution.py:46
  1232.7 19.6 %fusion.16 = f32[32,32]{1,0:T(8,128)S(1)} fusion(f32[8,16,2,32,4,128]{5,0,4,1,3,2:T(8,128)} %copy.85), kind=kOutput, calls=%fused_computation.14 | convolution fusion | flops 1610612736 | bytes 16781312 | tf_op jit(solution)/shard_map/xycoi,zycoi->xz/dot_general | solution.py:48
  1252.3 39.4 %psum.45 = f32[32,32]{1,0:T(8,128)S(1)} all-reduce(f32[32,32]{1,0:T(8,128)S(1)} %fusion.16), channel_id=1, replica_groups=mesh['fsdp'=8,'mode'=4] {'fsdp','mode'}, use_global_device_ids=true, to_apply=%region_5.9 | all-reduce | flops 1024 | bytes 8192 | tf_op jit(solution)/shard_map/psum | solution.py:47
  1292.0 1.5 cholesky.202
  1294.8 1.2 custom-call.26
  1296.6 1.5 cholesky.213
  1299.4 1.2 custom-call.27
  1300.8 4.3 fusion.8
  1305.1 3.3 copy.97
  1308.7 1.3 fusion.81
  1310.5 11.7 cholesky.180
  1323.6 9.8 custom-call.24
  1333.7 1.3 fusion.83
  1335.6 11.7 cholesky.191
  1348.6 10.0 custom-call.25
  1358.9 26.3 %reduce-scatter.3.cloned.1.call-done = f32[4,8,2,32,128]{4,3,2,1,0:T(8,128)} async-done(((f32[16,8,2,32,128]{4,3,2,1,0:T(8,128)}), f32[4,8,2,32,128]{4,3,2,1,0:T(8,128)}) %reduce-scatter.3.cloned.1.call-update) | async-done | bytes 1048592 | tf_op jit(solution)/shard_map/reduce_scatter | solution.py:57
  1385.3 6.7 fusion.45
  1392.0 0.9 dynamic-slice_bitcast_fusion
  1394.2 49.6 %reduce-scatter.5.cloned.1.call-done = f32[16,4,8,2,128]{4,0,3,2,1:T(8,128)} async-done(((f32[128,4,8,2,128]{4,0,3,2,1:T(8,128)}), f32[16,4,8,2,128]{4,0,3,2,1:T(8,128)}) %reduce-scatter.5.cloned.1.call-update) | async-done | bytes 524304 | tf_op jit(solution)/shard_map/reduce_scatter | solution.py:64
  1443.7 2.1 copy.99
  (93 shorter events, 20.8 us)
Async XLA Ops:
  8.0 785.4 %copy-start = (f32[512,128]{1,0:T(8,128)S(1)}, f32[512,128]{1,0:T(8,128)}, u32[]{:S(2)}) copy-start(f32[512,128]{1,0:T(8,128)} %param.17) | copy-start | bytes 786436
  125.4 190.4 %all-to-all-start = ((f32[8,1,524288]{2,1,0:T(1,128)}), f32[8,1,524288]{2,1,0:T(1,128)}, u32[]{:S(2)}, u32[]{:S(2)}) async-start(f32[8,1,524288]{2,1,0:T(1,128)} %reshape.45), calls=%async_computation | async-start | bytes 33554432 | tf_op jit(solution)/shard_map/all_to_all | solution.py:42
  315.8 743.6 %all-to-all-start.1 = ((f32[4,1,1048576]{2,1,0:T(1,128)}), f32[4,1,1048576]{2,1,0:T(1,128)}, u32[]{:S(2)}, u32[]{:S(2)}) async-start(f32[4,1,1048576]{2,1,0:T(1,128)} %reshape.47), calls=%async_computation.1 | async-start | bytes 33554432 | tf_op jit(solution)/shard_map/all_to_all | solution.py:46
  323.0 324.9 %all-reduce.4.cloned.1.call-start = ((), (), s32[]{:S(2)}) async-start(), calls=%async_computation.4 | async-start | bytes 2097152 | tf_op jit(solution)/shard_map/psum | solution.py:15
  354.6 288.9 %copy-start.7 = (f32[16,8]{0,1:T(8,128)S(1)}, f32[16,8]{0,1:T(8,128)}, u32[]{:S(2)}) copy-start(f32[16,8]{0,1:T(8,128)} %param.20) | copy-start | bytes 1540
  354.7 438.7 %all-reduce.6.cloned.1.call-start = ((), (), s32[]{:S(2)}) async-start(), calls=%async_computation.5 | async-start | bytes 2097152 | tf_op jit(solution)/shard_map/psum | solution.py:15
  647.9 660.8 %all-reduce.8.cloned.1.call-start = ((), (), s32[]{:S(2)}) async-start(), calls=%async_computation.6 | async-start | bytes 524288 | tf_op jit(solution)/shard_map/psum | solution.py:43
  650.3 217.6 %copy-start.5 = (f32[8,16]{1,0:T(8,128)}, f32[8,16]{1,0:T(8,128)S(1)}, u32[]{:S(2)}) copy-start(f32[8,16]{1,0:T(8,128)S(1)} %fusion.64) | copy-start | bytes 1540
  846.2 0.7 copy-start.2
  1059.3 326.0 %reduce-scatter.3.cloned.1.call-start = ((), (), s32[]{:S(2)}) async-start(), calls=%async_computation.7 | async-start | bytes 5242880 | tf_op jit(solution)/shard_map/reduce_scatter | solution.py:57
  1232.7 59.0 %copy-start.6 = (f32[32,16]{0,1:T(8,128)S(1)}, f32[32,16]{0,1:T(8,128)}, u32[]{:S(2)}) copy-start(f32[32,16]{0,1:T(8,128)} %param.19) | copy-start | bytes 6148
  1232.7 76.0 %copy-start.3 = (f32[256,128]{1,0:T(8,128)S(1)}, f32[256,128]{1,0:T(8,128)}, u32[]{:S(2)}) copy-start(f32[256,128]{1,0:T(8,128)} %param.18) | copy-start | bytes 393220
  1232.7 213.2 %copy-start.1 = (f32[512,128]{1,0:T(8,128)S(1)}, f32[512,128]{1,0:T(8,128)}, u32[]{:S(2)}) copy-start(f32[512,128]{1,0:T(8,128)} %param.17) | copy-start | bytes 786436
  1300.8 145.0 %copy-start.4 = (f32[16,32]{1,0:T(8,128)}, f32[16,32]{1,0:T(8,128)S(1)}, u32[]{:S(2)}) copy-start(f32[16,32]{1,0:T(8,128)S(1)} %fusion.51) | copy-start | bytes 6148
  1308.4 135.4 %reduce-scatter.5.cloned.1.call-start = ((), (), s32[]{:S(2)}) async-start(), calls=%async_computation.8 | async-start | bytes 4718592 | tf_op jit(solution)/shard_map/reduce_scatter | solution.py:64
Sparse Core Ops, SparseCore 0:
  354.8 128.8 all-reduce.3
  648.0 145.2 all-reduce.5
  1308.5 76.7 reduce-scatter.2
  1392.1 51.6 reduce-scatter.4
Sparse Core Ops, SparseCore 1:
  1059.4 125.2 all-reduce.7
